TPU v7x, 32 devices: a whole 2x2x4 slice. The times are simulated.
32 devices in a mesh: grp: 2 (over y), head: 16 (over z, x, core).
Axes of the slice: x: 2, y: 2, z: 4, core: 2. Of those that a mesh axis runs over, the one named last changes fastest.
Arguments:
- queries: bfloat16 [32, 16, 576], P('grp', 'head'), parts along dimension 0, may hold values from -32 to 32
- kv_pages: bfloat16 [16384, 64, 576], P(('grp', 'head')), parts along dimension 0, may hold values from -8 to 8
- page_table: int32 [32, 512], P('grp'), parts along dimension 0, may hold values from 0 to 8191, as said below
- lengths: int32 [32], P('grp'), parts along dimension 0, may hold values from 2048 to 32768
- selected: int32 [32, 32], P('grp'), parts along dimension 0, may hold values from 0 to 511, as said below
Outputs:
- attended: bfloat16 [32, 16, 512], P('grp', 'head'), parts along dimension 0
There are 2 independent parts, one for each index of `grp`. A program takes and returns all parts, laid end to end along the dimension named above; each array names one. Nothing has to cross between parts.
Inputs may be any that keep to these rules, and one draw needn't show every extreme that they name: `page_table`: every block of every request names a different page of the pool; the pages named by selected blocks fall at most 96 into one aligned run of 512 pages (one device's share of the pool), and some run holds exactly 96 of them. `selected`: each row names 32 different blocks of its request below ceil(lengths / 64); the first is the last such block.
All inputs are finite; a program needn't handle non-finite values.
Results may differ from a plain program's by a relative error of at most 0.0034.
Values may be sent and summed in bfloat16 or wider, within the bound.
No kernel may reach another device: no remote copies, remote signals or barrier semaphores. Data moves between devices by JAX's collectives and lax.ppermute only.
A program may use at most 128 MiB of HBM per device.

v0:
```python
import math
import jax
import jax.numpy as jnp
from jax import lax
from jax.sharding import PartitionSpec as P

ROPE = 64
SOFTMAX_SCALE = (0.1 * math.log(40.0) + 1.0) ** 2 / math.sqrt(192.0)


def local(queries, kv_pages, page_table, lengths, selected):
    channels = queries.shape[2]
    latent = channels - ROPE
    requests, pick_count = selected.shape
    pages_dev, page_len = (kv_pages.shape[0], kv_pages.shape[1])
    devices = lax.axis_size("head")
    capacity = 3 * requests * pick_count // devices
    own_index = lax.axis_index("head")
    all_queries = lax.all_gather(queries, "head", axis=1, tiled=True)
    page_ids = jnp.take_along_axis(page_table, selected, axis=1).reshape(-1)
    mine_mask = page_ids // pages_dev == own_index
    pair_count = requests * pick_count
    order_key = jnp.where(mine_mask, 0, pair_count) + jnp.arange(pair_count, dtype=jnp.int32)
    slot_ids = jnp.argsort(order_key)[:capacity]
    slot_live = mine_mask[slot_ids]
    slot_request = slot_ids // pick_count
    slot_block = selected.reshape(-1)[slot_ids]
    local_page = jnp.where(slot_live, page_ids[slot_ids] - own_index * pages_dev, 0)
    blocks = kv_pages[local_page]
    positions = slot_block[:, None] * page_len + jnp.arange(page_len, dtype=jnp.int32)[None, :]
    live_mask = slot_live[:, None] & (positions < lengths[slot_request][:, None])
    slot_queries = all_queries[slot_request]
    scores = (
        jnp.einsum("chd,ctd->cht", slot_queries, blocks, preferred_element_type=jnp.float32)
        * SOFTMAX_SCALE
    )
    masked = jnp.where(live_mask[:, None, :], scores, jnp.float32(-1e30))
    slot_top = jnp.max(masked, axis=2)
    owner_mask = slot_request[:, None] == jnp.arange(requests, dtype=jnp.int32)[None, :]
    local_top = jnp.max(
        jnp.where(owner_mask[:, :, None], slot_top[:, None, :], jnp.float32(-1e30)), axis=0
    )
    row_top = lax.pmax(local_top, "head")
    weights = jnp.where(
        live_mask[:, None, :], jnp.exp(masked - row_top[slot_request][:, :, None]), jnp.float32(0.0)
    )
    onehot = owner_mask.astype(jnp.float32)
    totals = jnp.einsum(
        "cr,ch->rh", onehot, jnp.sum(weights, axis=2), precision=lax.Precision.HIGHEST
    )
    slot_numer = jnp.einsum(
        "cht,cte->che",
        weights.astype(jnp.bfloat16),
        blocks[:, :, :latent],
        preferred_element_type=jnp.float32,
    )
    numer_sum = jnp.einsum("cr,che->rhe", onehot, slot_numer, precision=lax.Precision.HIGHEST)
    numer_own, totals_own = (
        lax.psum_scatter(numer_sum, "head", scatter_dimension=1, tiled=True),
        lax.psum_scatter(totals, "head", scatter_dimension=1, tiled=True),
    )
    return (numer_own / totals_own[:, :, None]).astype(jnp.bfloat16)


def solution(mesh):
    return jax.shard_map(
        local,
        mesh=mesh,
        in_specs=(
            P("grp", "head", None),
            P(("grp", "head"), None, None),
            P("grp", None),
            P("grp"),
            P("grp", None),
        ),
        out_specs=P("grp", "head", None),
        check_vma=False,
    )
```

profile of v0, /device:TPU:0, one launch (start us, length us, event | category | flops | bytes accessed | tf_op | source)
XLA Modules:
  0.0 230.6 jit_solution(13203962640777853632)
XLA Ops:
  6.5 0.0 copy-start
  6.5 0.0 copy-start.2
  6.5 0.0 reduce-scatter.2.cloned.1.call-start
  6.5 0.8 bitcast_or_fusion
  7.3 0.8 reshape.115
  8.1 1.9 fusion.22
  10.0 0.1 reshape.187
  10.1 0.0 copy-done
  10.1 4.5 %gather_fusion.6 = s32[512]{0:T(512)S(1)} fusion(s32[16,512]{1,0:T(8,128)S(1)} %copy-done, s32[512]{0:T(512)S(1)} %reshape.187), kind=kCustom, calls=%fused_computation.6 | custom fusion | bytes 8192 | tf_op jit(solution)/shard_map/jit(take_along_axis)/gather | solution.py:20
  14.6 0.1 reshape.190
  14.7 0.0 copy-done.2
  14.7 0.1 select_n.73
  14.8 3.8 %sort.17 = (s32[512]{0:T(512)}, s32[512]{0:T(512)S(1)}) sort(s32[512]{0:T(512)S(1)} %get-tuple-element.9, s32[512]{0:T(512)S(1)} %iota.23), dimensions={0}, to_apply=%region_0.0 | sort | flops 4608 | bytes 8192 | tf_op jit(solution)/shard_map/jit(argsort)/sort | solution.py:24
  18.6 9.9 %compare_select_fusion.3 = (s32[96]{0:T(128)S(1)}, s32[96]{0:T(128)S(1)}, s32[96]{0:T(128)S(1)}) fusion(s32[]{:T(128)} %bitcast.2, s32[]{:T(128)} %bitcast.3, s32[]{:T(128)} %bitcast.4, s32[]{:T(128)} %bitcast.5, s32[]{:T(128)} %bitcast.6, s32[]{:T(128)} %bitcast.7, s32[]{:T(128)} %bitcast.8, s32[]{:T(128)} %bitcast.9, s32[]{:T(128)} %bitcast.10, ...), kind=kLoop, calls=%fused_computation.45 | loop fusion | flops 4800 | bytes 1600 | tf_op jit(solution)/shard_map/gather | solution.py:31
  28.6 1.3 gather_fusion.3
  29.8 1.2 gather_fusion
  31.1 0.0 copy-start.3
  31.1 55.1 %copy.20 = bf16[512,64,576]{2,1,0:T(8,128)(2,1)} copy(bf16[512,64,576]{0,2,1:T(8,128)(2,1)} %param.6) | data formatting | bytes 75497472 | tf_op args[1]
  86.2 0.0 copy-done.3
  86.2 24.0 %all_gather.3 = bf16[16,16,576]{2,0,1:T(8,128)(2,1)S(1)} all-gather(bf16[16,1,576]{2,0,1:T(8,128)(2,1)S(1)} %copy-done.3), channel_id=1, replica_groups=mesh['grp'=2,'head'=16] {'head'}, dimensions={1}, use_global_device_ids=true | all-gather | bytes 313344 | tf_op jit(solution)/shard_map/all_gather | solution.py:19
  110.2 0.1 copy.19
  110.3 1.3 gather_fusion.1
  111.6 12.2 %gather_fusion.4 = bf16[96,64,576]{2,1,0:T(8,128)(2,1)} fusion(bf16[512,64,576]{2,1,0:T(8,128)(2,1)} %copy.20, s32[1024]{0:T(1024)S(1)} %pad_clamp_fusion), kind=kCustom, calls=%fused_computation.4 | custom fusion | bytes 14156160 | tf_op jit(solution)/shard_map/gather | solution.py:29
  123.8 0.9 gather_fusion.2
  124.8 0.1 fusion.11
  124.9 4.9 %fusion.23 = (f32[96,16]{1,0:T(8,128)S(1)}, f32[96,16,64]{2,1,0:T(8,128)S(1)}) fusion(bf16[96,16,576]{2,1,0:T(8,128)(2,1)S(1)} %gather_fusion.2, bf16[96,64,576]{2,1,0:T(8,128)(2,1)} %gather_fusion.4, pred[96,64]{1,0:T(8,128)(4,1)S(1)} %fusion.11), kind=kOutput, calls=%fused_computation.70 | convolution fusion | flops 113539584 | bytes 9252864 | tf_op jit(solution)/shard_map/chd,ctd->cht/dot_general | solution.py:34
  129.8 0.1 copy.21
  129.9 0.1 select_reduce_fusion
  130.0 30.3 %pmax.7 = f32[16,16]{1,0:T(8,128)S(1)} all-reduce(f32[16,16]{1,0:T(8,128)S(1)} %select_reduce_fusion), channel_id=1, replica_groups=mesh['grp'=2,'head'=16] {'head'}, use_global_device_ids=true, to_apply=%region_3.4 | all-reduce | flops 256 | bytes 2048 | tf_op jit(solution)/shard_map/pmax | solution.py:43
  160.3 0.6 gather_fusion.5
  161.0 0.0 copy-start.1
  161.0 0.0 copy-start.4
  161.0 3.8 %fusion = f32[96,16,512]{2,1,0:T(8,128)S(1)} fusion(bf16[96,64,576]{2,1,0:T(8,128)(2,1)} %gather_fusion.4, f32[96,16,64]{2,1,0:T(8,128)S(1)} %get-tuple-element.29, f32[96,16]{1,0:T(8,128)S(1)} %gather_fusion.5, pred[96,64]{1,0:T(8,128)(4,1)S(1)} %fusion.11), kind=kOutput, calls=%fused_computation.7 | convolution fusion | flops 100958208 | bytes 9842688 | tf_op jit(solution)/shard_map/cht,cte->che/dot_general | solution.py:51
  164.8 3.7 %fusion.2 = f32[16,16,512]{2,0,1:T(8,128)} fusion(f32[96,16,512]{2,1,0:T(8,128)S(1)} %fusion, s32[96]{0:T(128)S(1)} %get-tuple-element.8), kind=kOutput, calls=%fused_computation.9 | convolution fusion | flops 150996480 | bytes 3670400 | tf_op jit(solution)/shard_map/cr,che->rhe/dot_general | solution.py:57
  168.5 0.0 reduce-scatter.2.cloned.1.call-update
  168.5 0.0 copy-done.4
  168.5 0.6 dynamic-slice
  169.1 0.5 fusion.5
  169.6 0.2 fusion.13
  169.8 30.1 %all-reduce = f32[16,16]{0,1:T(8,128)S(1)} all-reduce(f32[16,16]{0,1:T(8,128)S(1)} %fusion.13), channel_id=3, replica_groups=mesh['grp'=2,'head'=16] {'head'}, use_global_device_ids=true, to_apply=%region_6.7.clone | all-reduce | flops 256 | bytes 2048
  200.0 0.7 dynamic-slice_bitcast_fusion
  200.6 21.7 %reduce-scatter.2.cloned.1.call-done = f32[16,1,512]{2,0,1:T(8,128)} async-done(((f32[16,16,512]{2,0,1:T(8,128)}), f32[16,1,512]{2,0,1:T(8,128)}) %reduce-scatter.2.cloned.1.call-update) | async-done | bytes 32784 | tf_op jit(solution)/shard_map/reduce_scatter | solution.py:59
  222.3 1.4 divide_convert_fusion
  223.8 0.0 copy-done.1
  (10 shorter events, 0.1 us)
Async XLA Ops:
  6.5 3.6 %copy-start = (s32[16,512]{1,0:T(8,128)S(1)}, s32[16,512]{1,0:T(8,128)}, u32[]{:S(2)}) copy-start(s32[16,512]{1,0:T(8,128)} %param.7) | copy-start | bytes 98308
  6.5 8.2 %copy-start.2 = (s32[16,32]{1,0:T(8,128)S(1)}, s32[16,32]{1,0:T(8,128)}, u32[]{:S(2)}) copy-start(s32[16,32]{1,0:T(8,128)} %param.9) | copy-start | bytes 6148
  6.5 215.8 %reduce-scatter.2.cloned.1.call-start = ((), (), s32[]{:S(2)}) async-start(), calls=%async_computation.1 | async-start | bytes 557056 | tf_op jit(solution)/shard_map/reduce_scatter | solution.py:59
  31.1 55.1 %copy-start.3 = (bf16[16,1,576]{2,0,1:T(8,128)(2,1)S(1)}, bf16[16,1,576]{2,0,1:T(8,128)(2,1)}, u32[]{:S(2)}) copy-start(bf16[16,1,576]{2,0,1:T(8,128)(2,1)} %param.5) | copy-start | bytes 55300
  161.0 62.8 %copy-start.1 = (s32[16,512]{1,0:T(8,128)S(1)}, s32[16,512]{1,0:T(8,128)}, u32[]{:S(2)}) copy-start(s32[16,512]{1,0:T(8,128)} %param.7) | copy-start | bytes 98308
  161.0 7.5 %copy-start.4 = (u32[32]{0:T(128)S(1)}, u32[32]{0:T(128)}, u32[]{:S(2)}) copy-start(u32[32]{0:T(128)} %constant.94) | copy-start | bytes 388
Sparse Core Ops, SparseCore 0:
  168.6 53.6 reduce-scatter.1
where the time goes:
time: 233 us; the launch traced here: 231 us
  blocking collectives  84.4 us (36%)
  local copies, waits for them, and re-layouts  81.5 us (35%)
  waiting for transfers between devices  21.7 us (9%)
  other arithmetic  16.7 us (7%)
  between operations  13.6 us (6%)
  matrix products  12.6 us (5%)
    unnamed x12, local copies, waits for them, and re-layouts  55.7 us
    pmax x1, blocking collectives, local(): row_top = lax.pmax(local_top, 'head')  30.3 us
    unnamed x1, blocking collectives  30.1 us
    all_gather x1, blocking collectives, local(): all_queries = lax.all_gather(queries, 'head', axis=1, tiled=True)  24 us
    reduce_scatter x1, waiting for transfers between devices, local(): lax.psum_scatter(numer_sum, 'head', scatter_dimension=1, tiled=True)  21.7 us
    gather x1, local copies, waits for them, and re-layouts, local(): blocks = kv_pages[local_page]  12.2 us
    gather x1, other arithmetic, local(): lengths[slot_request][:, None]  9.93 us
    dot_general x1, matrix products, local(): jnp.einsum('chd,ctd->cht', slot_queries, blocks, preferred_element_type=j...  4.93 us
  transfers between devices with their start and end apart: 1, of which 1 were waited for; matrix products, arithmetic and copies ran while one was open for 1% of the time, Pallas kernels for 0%

commit v1 on v0

--- a/solution.py
+++ b/solution.py
@@ -8,6 +8,19 @@
 SOFTMAX_SCALE = (0.1 * math.log(40.0) + 1.0) ** 2 / math.sqrt(192.0)
 
 
+def ring_gather(shard, axis, dim):
+    count, index, rows = (lax.axis_size(axis), lax.axis_index(axis), shard.shape[dim])
+    right = [(i, (i + 1) % count) for i in range(count)]
+    out = jnp.zeros((*shard.shape[:dim], count * rows, *shard.shape[dim + 1 :]), shard.dtype)
+    carried = shard
+    for step in range(count):
+        owner = (index - step) % count
+        out = lax.dynamic_update_slice_in_dim(out, carried, owner * rows, axis=dim)
+        if step < count - 1:
+            carried = lax.ppermute(carried, axis, right)
+    return out
+
+
 def local(queries, kv_pages, page_table, lengths, selected):
     channels = queries.shape[2]
     latent = channels - ROPE
@@ -16,7 +29,7 @@
     devices = lax.axis_size("head")
     capacity = 3 * requests * pick_count // devices
     own_index = lax.axis_index("head")
-    all_queries = lax.all_gather(queries, "head", axis=1, tiled=True)
+    all_queries = ring_gather(queries, "head", 1)
     page_ids = jnp.take_along_axis(page_table, selected, axis=1).reshape(-1)
     mine_mask = page_ids // pages_dev == own_index
     pair_count = requests * pick_count

time: 233 us -> 294 us (1.26)
  waiting for transfers between devices: 21.7 us -> 86.6 us
  blocking collectives: 84.4 us -> 64.4 us
  local copies, waits for them, and re-layouts: 81.5 us -> 97.3 us
    ppermute x0 -> x15, waiting for transfers between devices: none -> 66.1 us  [ring_gather(): carried = lax.ppermute(carried, axis, right)]
    all_gather x1 -> x0, blocking collectives: 24 us -> none  [local(): all_queries = lax.all_gather(queries, 'head', axis=1, tiled=True)]
    dynamic_update_slice x0 -> x16, local copies, waits for them, and re-layouts: none -> 17 us  [ring_gather(): out = lax.dynamic_update_slice_in_dim(out, carried, owner * rows, axis=dim)]
    pmax x1, blocking collectives: 30.3 us -> 34.4 us  [local(): row_top = lax.pmax(local_top, 'head')]
    unnamed x12 -> x13, local copies, waits for them, and re-layouts: 55.7 us -> 56.5 us
  transfers between devices with their start and end apart: 1 -> 16, of which waited for: 1 -> 14; matrix products, arithmetic and copies ran while one was open for 1% -> 37% of each run, Pallas kernels for 0% -> 0%
where the time goes in v1:
time: 294 us; the launch traced here: 292 us
  local copies, waits for them, and re-layouts  97.3 us (33%)
  waiting for transfers between devices  86.6 us (29%)
  blocking collectives  64.4 us (22%)
  other arithmetic  16.7 us (6%)
  between operations  14.1 us (5%)
  matrix products  12.7 us (4%)
    ppermute x15, waiting for transfers between devices, ring_gather(): carried = lax.ppermute(carried, axis, right)  66.1 us
    unnamed x13, local copies, waits for them, and re-layouts  56.5 us
    pmax x1, blocking collectives, local(): row_top = lax.pmax(local_top, 'head')  34.4 us
    unnamed x1, blocking collectives  30 us
    reduce_scatter x1, waiting for transfers between devices, local(): lax.psum_scatter(numer_sum, 'head', scatter_dimension=1, tiled=True)  20.5 us
    dynamic_update_slice x16, local copies, waits for them, and re-layouts, ring_gather(): out = lax.dynamic_update_slice_in_dim(out, carried, owner * rows, axis=dim)  17 us
    gather x1, local copies, waits for them, and re-layouts, local(): blocks = kv_pages[local_page]  12.1 us
    gather x1, other arithmetic, local(): lengths[slot_request][:, None]  9.94 us
  transfers between devices with their start and end apart: 16, of which 14 were waited for; matrix products, arithmetic and copies ran while one was open for 37% of the time, Pallas kernels for 0%

profile of v1, /device:TPU:0, one launch (start us, length us, event | category | flops | bytes accessed | tf_op | source)
XLA Modules:
  0.0 292.4 jit_solution(6333831035126092836)
XLA Ops:
  6.5 0.8 copy.21
  7.3 0.5 collective-permute-start
  7.9 6.6 %collective-permute-done = bf16[16,1,576]{2,1,0:T(2,128)(2,1)S(1)} collective-permute-done((bf16[16,1,576]{2,1,0:T(2,128)(2,1)S(1)}, bf16[16,1,576]{2,1,0:T(2,128)(2,1)S(1)}, u32[]{:S(2)}, u32[]{:S(2)}) %collective-permute-start) | collective-permute-done | bytes 18464 | tf_op jit(solution)/shard_map/ppermute | solution.py:20
  14.5 6.1 %collective-permute-done.1 = bf16[16,1,576]{2,1,0:T(2,128)(2,1)S(1)} collective-permute-done((bf16[16,1,576]{2,1,0:T(2,128)(2,1)S(1)}, bf16[16,1,576]{2,1,0:T(2,128)(2,1)S(1)}, u32[]{:S(2)}, u32[]{:S(2)}) %collective-permute-start.1) | collective-permute-done | bytes 18464 | tf_op jit(solution)/shard_map/ppermute | solution.py:20
  20.7 0.7 bitcast_or_fusion
  21.4 0.1 reshape.187
  21.4 4.5 %gather_fusion.6 = s32[512]{0:T(512)S(1)} fusion(s32[16,512]{1,0:T(8,128)S(1)} %copy-done, s32[512]{0:T(512)S(1)} %reshape.187), kind=kCustom, calls=%fused_computation.6 | custom fusion | bytes 8192 | tf_op jit(solution)/shard_map/jit(take_along_axis)/gather | solution.py:33
  26.0 0.1 reshape.190
  26.0 0.7 collective-permute-done.2
  26.8 0.1 select_n.188
  26.9 6.0 %collective-permute-done.3 = bf16[16,1,576]{2,1,0:T(2,128)(2,1)S(1)} collective-permute-done((bf16[16,1,576]{2,1,0:T(2,128)(2,1)S(1)}, bf16[16,1,576]{2,1,0:T(2,128)(2,1)S(1)}, u32[]{:S(2)}, u32[]{:S(2)}) %collective-permute-start.3) | collective-permute-done | bytes 18464 | tf_op jit(solution)/shard_map/ppermute | solution.py:20
  32.9 6.1 %collective-permute-done.4 = bf16[16,1,576]{2,1,0:T(2,128)(2,1)S(1)} collective-permute-done((bf16[16,1,576]{2,1,0:T(2,128)(2,1)S(1)}, bf16[16,1,576]{2,1,0:T(2,128)(2,1)S(1)}, u32[]{:S(2)}, u32[]{:S(2)}) %collective-permute-start.4) | collective-permute-done | bytes 18464 | tf_op jit(solution)/shard_map/ppermute | solution.py:20
  39.0 0.7 fusion.22
  39.7 3.8 %sort.17 = (s32[512]{0:T(512)}, s32[512]{0:T(512)S(1)}) sort(s32[512]{0:T(512)S(1)} %get-tuple-element.9, s32[512]{0:T(512)S(1)} %iota.23), dimensions={0}, to_apply=%region_0.1 | sort | flops 4608 | bytes 8192 | tf_op jit(solution)/shard_map/jit(argsort)/sort | solution.py:37
  43.5 1.6 collective-permute-done.5
  45.2 9.9 %compare_select_fusion.3 = (s32[96]{0:T(128)S(1)}, s32[96]{0:T(128)S(1)}, s32[96]{0:T(128)S(1)}) fusion(s32[]{:T(128)} %bitcast.2, s32[]{:T(128)} %bitcast.3, s32[]{:T(128)} %bitcast.4, s32[]{:T(128)} %bitcast.5, s32[]{:T(128)} %bitcast.6, s32[]{:T(128)} %bitcast.7, s32[]{:T(128)} %bitcast.8, s32[]{:T(128)} %bitcast.9, s32[]{:T(128)} %bitcast.10, ...), kind=kLoop, calls=%fused_computation.45 | loop fusion | flops 4800 | bytes 1600 | tf_op jit(solution)/shard_map/gather | solution.py:44
  55.1 0.1 collective-permute-start.7
  55.2 0.1 reshape.115
  55.3 1.3 gather_fusion.1
  56.5 4.7 %collective-permute-done.7 = bf16[16,1,576]{2,1,0:T(2,128)(2,1)S(1)} collective-permute-done((bf16[16,1,576]{2,1,0:T(2,128)(2,1)S(1)}, bf16[16,1,576]{2,1,0:T(2,128)(2,1)S(1)}, u32[]{:S(2)}, u32[]{:S(2)}) %collective-permute-start.7) | collective-permute-done | bytes 18464 | tf_op jit(solution)/shard_map/ppermute | solution.py:20
  61.3 1.2 gather_fusion
  62.5 4.9 %collective-permute-done.8 = bf16[16,1,576]{2,1,0:T(2,128)(2,1)S(1)} collective-permute-done((bf16[16,1,576]{2,1,0:T(2,128)(2,1)S(1)}, bf16[16,1,576]{2,1,0:T(2,128)(2,1)S(1)}, u32[]{:S(2)}, u32[]{:S(2)}) %collective-permute-start.8) | collective-permute-done | bytes 18464 | tf_op jit(solution)/shard_map/ppermute | solution.py:20
  67.4 0.1 fusion.11
  67.5 6.0 %collective-permute-done.9 = bf16[16,1,576]{2,1,0:T(2,128)(2,1)S(1)} collective-permute-done((bf16[16,1,576]{2,1,0:T(2,128)(2,1)S(1)}, bf16[16,1,576]{2,1,0:T(2,128)(2,1)S(1)}, u32[]{:S(2)}, u32[]{:S(2)}) %collective-permute-start.9) | collective-permute-done | bytes 18464 | tf_op jit(solution)/shard_map/ppermute | solution.py:20
  73.6 1.3 gather_fusion.3
  74.8 4.8 %collective-permute-done.10 = bf16[16,1,576]{2,1,0:T(2,128)(2,1)S(1)} collective-permute-done((bf16[16,1,576]{2,1,0:T(2,128)(2,1)S(1)}, bf16[16,1,576]{2,1,0:T(2,128)(2,1)S(1)}, u32[]{:S(2)}, u32[]{:S(2)}) %collective-permute-start.10) | collective-permute-done | bytes 18464 | tf_op jit(solution)/shard_map/ppermute | solution.py:20
  79.7 6.1 %collective-permute-done.11 = bf16[16,1,576]{2,1,0:T(2,128)(2,1)S(1)} collective-permute-done((bf16[16,1,576]{2,1,0:T(2,128)(2,1)S(1)}, bf16[16,1,576]{2,1,0:T(2,128)(2,1)S(1)}, u32[]{:S(2)}, u32[]{:S(2)}) %collective-permute-start.11) | collective-permute-done | bytes 18464 | tf_op jit(solution)/shard_map/ppermute | solution.py:20
  85.8 6.1 %collective-permute-done.12 = bf16[16,1,576]{2,1,0:T(2,128)(2,1)S(1)} collective-permute-done((bf16[16,1,576]{2,1,0:T(2,128)(2,1)S(1)}, bf16[16,1,576]{2,1,0:T(2,128)(2,1)S(1)}, u32[]{:S(2)}, u32[]{:S(2)}) %collective-permute-start.12) | collective-permute-done | bytes 18464 | tf_op jit(solution)/shard_map/ppermute | solution.py:20
  91.9 6.1 %collective-permute-done.13 = bf16[16,1,576]{2,1,0:T(2,128)(2,1)S(1)} collective-permute-done((bf16[16,1,576]{2,1,0:T(2,128)(2,1)S(1)}, bf16[16,1,576]{2,1,0:T(2,128)(2,1)S(1)}, u32[]{:S(2)}, u32[]{:S(2)}) %collective-permute-start.13) | collective-permute-done | bytes 18464 | tf_op jit(solution)/shard_map/ppermute | solution.py:20
  98.3 55.1 %copy.23 = bf16[512,64,576]{2,1,0:T(8,128)(2,1)} copy(bf16[512,64,576]{0,2,1:T(8,128)(2,1)} %param.6) | data formatting | bytes 75497472 | tf_op args[1]
  153.4 12.1 %gather_fusion.4 = bf16[96,64,576]{2,1,0:T(8,128)(2,1)} fusion(bf16[512,64,576]{2,1,0:T(8,128)(2,1)} %copy.23, s32[1024]{0:T(1024)S(1)} %pad_clamp_fusion), kind=kCustom, calls=%fused_computation.4 | custom fusion | bytes 14156160 | tf_op jit(solution)/shard_map/gather | solution.py:42
  165.6 1.1 dynamic_update_slice.48
  166.8 1.1 dynamic_update_slice.49
  167.8 1.1 dynamic_update_slice.50
  168.9 1.1 dynamic_update_slice.51
  170.0 1.1 dynamic_update_slice.52
  171.1 1.1 dynamic_update_slice.53
  172.1 1.1 dynamic_update_slice.54
  173.2 1.1 dynamic_update_slice.55
  174.3 1.1 dynamic_update_slice.56
  175.3 1.1 dynamic_update_slice.57
  176.4 1.1 dynamic_update_slice.58
  177.5 1.1 dynamic_update_slice.59
  178.6 1.1 dynamic_update_slice.60
  179.6 1.1 dynamic_update_slice.61
  180.7 1.1 dynamic_update_slice.62
  181.8 1.1 dynamic_update_slice.63
  182.9 0.9 gather_fusion.2
  183.8 5.0 %fusion.23 = (f32[96,16]{1,0:T(8,128)S(1)}, f32[96,16,64]{2,1,0:T(8,128)S(1)}) fusion(bf16[96,16,576]{2,1,0:T(8,128)(2,1)S(1)} %gather_fusion.2, bf16[96,64,576]{2,1,0:T(8,128)(2,1)} %gather_fusion.4, pred[96,64]{1,0:T(8,128)(4,1)S(1)} %fusion.11), kind=kOutput, calls=%fused_computation.70 | convolution fusion | flops 113539584 | bytes 9252864 | tf_op jit(solution)/shard_map/chd,ctd->cht/dot_general | solution.py:47
  188.8 0.1 copy.24
  188.9 0.1 select_reduce_fusion
  189.0 34.4 %pmax.7 = f32[16,16]{1,0:T(8,128)S(1)} all-reduce(f32[16,16]{1,0:T(8,128)S(1)} %select_reduce_fusion), channel_id=1, replica_groups=mesh['grp'=2,'head'=16] {'head'}, use_global_device_ids=true, to_apply=%region_3.4 | all-reduce | flops 256 | bytes 2048 | tf_op jit(solution)/shard_map/pmax | solution.py:56
  223.4 0.6 gather_fusion.5
  224.0 0.0 copy-start.4
  224.1 3.8 %fusion = f32[96,16,512]{2,1,0:T(8,128)S(1)} fusion(bf16[96,64,576]{2,1,0:T(8,128)(2,1)} %gather_fusion.4, f32[96,16,64]{2,1,0:T(8,128)S(1)} %get-tuple-element.29, f32[96,16]{1,0:T(8,128)S(1)} %gather_fusion.5, pred[96,64]{1,0:T(8,128)(4,1)S(1)} %fusion.11), kind=kOutput, calls=%fused_computation.7 | convolution fusion | flops 100958208 | bytes 9842688 | tf_op jit(solution)/shard_map/cht,cte->che/dot_general | solution.py:64
  227.9 3.7 %fusion.2 = f32[16,16,512]{2,0,1:T(8,128)} fusion(f32[96,16,512]{2,1,0:T(8,128)S(1)} %fusion, s32[96]{0:T(128)S(1)} %get-tuple-element.8), kind=kOutput, calls=%fused_computation.9 | convolution fusion | flops 150996480 | bytes 3670400 | tf_op jit(solution)/shard_map/cr,che->rhe/dot_general | solution.py:70
  231.6 0.0 reduce-scatter.2.cloned.1.call-update
  231.6 0.6 dynamic-slice
  232.2 0.5 fusion.5
  232.7 0.2 fusion.13
  232.9 30.0 %all-reduce = f32[16,16]{0,1:T(8,128)S(1)} all-reduce(f32[16,16]{0,1:T(8,128)S(1)} %fusion.13), channel_id=3, replica_groups=mesh['grp'=2,'head'=16] {'head'}, use_global_device_ids=true, to_apply=%region_6.7.clone | all-reduce | flops 256 | bytes 2048
  262.9 0.7 dynamic-slice_bitcast_fusion
  263.6 20.5 %reduce-scatter.2.cloned.1.call-done = f32[16,1,512]{2,0,1:T(8,128)} async-done(((f32[16,16,512]{2,0,1:T(8,128)}), f32[16,1,512]{2,0,1:T(8,128)}) %reduce-scatter.2.cloned.1.call-update) | async-done | bytes 32784 | tf_op jit(solution)/shard_map/reduce_scatter | solution.py:72
  284.1 1.4 divide_convert_fusion
  (36 shorter events, 0.1 us)
Async XLA Ops:
  6.5 14.9 %copy-start = (s32[16,512]{1,0:T(8,128)S(1)}, s32[16,512]{1,0:T(8,128)}, u32[]{:S(2)}) copy-start(s32[16,512]{1,0:T(8,128)} %param.7) | copy-start | bytes 98308
  6.5 20.2 %copy-start.3 = (s32[16,32]{1,0:T(8,128)S(1)}, s32[16,32]{1,0:T(8,128)}, u32[]{:S(2)}) copy-start(s32[16,32]{1,0:T(8,128)} %param.9) | copy-start | bytes 6148
  6.5 32.5 %copy-start.2 = (s32[16]{0:T(128)S(1)}, s32[16]{0:T(128)}, u32[]{:S(2)}) copy-start(s32[16]{0:T(128)} %param.8) | copy-start | bytes 196
  6.5 277.6 %reduce-scatter.2.cloned.1.call-start = ((), (), s32[]{:S(2)}) async-start(), calls=%async_computation.1 | async-start | bytes 557056 | tf_op jit(solution)/shard_map/reduce_scatter | solution.py:72
  7.3 7.2 %collective-permute-start = (bf16[16,1,576]{2,1,0:T(2,128)(2,1)S(1)}, bf16[16,1,576]{2,1,0:T(2,128)(2,1)S(1)}, u32[]{:S(2)}, u32[]{:S(2)}) collective-permute-start(bf16[16,1,576]{2,1,0:T(2,128)(2,1)S(1)} %copy.21), channel_id=1, source_target_pairs={{0,1},{1,2},{2,3},{3,4},{4,5},{5,6},{6,7},{7,8},{8,9},{9,10},{10,1... | collective-permute-start | bytes 55304 | tf_op jit(solution)/shard_map/ppermute | solution.py:20
  14.5 6.1 %collective-permute-start.1 = (bf16[16,1,576]{2,1,0:T(2,128)(2,1)S(1)}, bf16[16,1,576]{2,1,0:T(2,128)(2,1)S(1)}, u32[]{:S(2)}, u32[]{:S(2)}) collective-permute-start(bf16[16,1,576]{2,1,0:T(2,128)(2,1)S(1)} %collective-permute-done), channel_id=1, source_target_pairs={{0,1},{1,2},{2,3},{3,4},{4,5},{5,6},{6,7},{7,8},{8,9},{9,10},{10,1... | collective-permute-start | bytes 55304 | tf_op jit(solution)/shard_map/ppermute | solution.py:20
  20.7 6.1 %collective-permute-start.2 = (bf16[16,1,576]{2,1,0:T(2,128)(2,1)S(1)}, bf16[16,1,576]{2,1,0:T(2,128)(2,1)S(1)}, u32[]{:S(2)}, u32[]{:S(2)}) collective-permute-start(bf16[16,1,576]{2,1,0:T(2,128)(2,1)S(1)} %collective-permute-done.1), channel_id=1, source_target_pairs={{0,1},{1,2},{2,3},{3,4},{4,5},{5,6},{6,7},{7,8},{8,9},{9,10},{10,1... | collective-permute-start | bytes 55304 | tf_op jit(solution)/shard_map/ppermute | solution.py:20
  26.8 6.1 %collective-permute-start.3 = (bf16[16,1,576]{2,1,0:T(2,128)(2,1)S(1)}, bf16[16,1,576]{2,1,0:T(2,128)(2,1)S(1)}, u32[]{:S(2)}, u32[]{:S(2)}) collective-permute-start(bf16[16,1,576]{2,1,0:T(2,128)(2,1)S(1)} %collective-permute-done.2), channel_id=1, source_target_pairs={{0,1},{1,2},{2,3},{3,4},{4,5},{5,6},{6,7},{7,8},{8,9},{9,10},{10,1... | collective-permute-start | bytes 55304 | tf_op jit(solution)/shard_map/ppermute | solution.py:20
  32.9 6.1 %collective-permute-start.4 = (bf16[16,1,576]{2,1,0:T(2,128)(2,1)S(1)}, bf16[16,1,576]{2,1,0:T(2,128)(2,1)S(1)}, u32[]{:S(2)}, u32[]{:S(2)}) collective-permute-start(bf16[16,1,576]{2,1,0:T(2,128)(2,1)S(1)} %collective-permute-done.3), channel_id=1, source_target_pairs={{0,1},{1,2},{2,3},{3,4},{4,5},{5,6},{6,7},{7,8},{8,9},{9,10},{10,1... | collective-permute-start | bytes 55304 | tf_op jit(solution)/shard_map/ppermute | solution.py:20
  39.0 6.1 %collective-permute-start.5 = (bf16[16,1,576]{2,1,0:T(2,128)(2,1)S(1)}, bf16[16,1,576]{2,1,0:T(2,128)(2,1)S(1)}, u32[]{:S(2)}, u32[]{:S(2)}) collective-permute-start(bf16[16,1,576]{2,1,0:T(2,128)(2,1)S(1)} %collective-permute-done.4), channel_id=1, source_target_pairs={{0,1},{1,2},{2,3},{3,4},{4,5},{5,6},{6,7},{7,8},{8,9},{9,10},{10,1... | collective-permute-start | bytes 55304 | tf_op jit(solution)/shard_map/ppermute | solution.py:20
  45.2 10.0 %collective-permute-start.6 = (bf16[16,1,576]{2,1,0:T(2,128)(2,1)S(1)}, bf16[16,1,576]{2,1,0:T(2,128)(2,1)S(1)}, u32[]{:S(2)}, u32[]{:S(2)}) collective-permute-start(bf16[16,1,576]{2,1,0:T(2,128)(2,1)S(1)} %collective-permute-done.5), channel_id=1, source_target_pairs={{0,1},{1,2},{2,3},{3,4},{4,5},{5,6},{6,7},{7,8},{8,9},{9,10},{10,1... | collective-permute-start | bytes 55304 | tf_op jit(solution)/shard_map/ppermute | solution.py:20
  55.1 6.2 %collective-permute-start.7 = (bf16[16,1,576]{2,1,0:T(2,128)(2,1)S(1)}, bf16[16,1,576]{2,1,0:T(2,128)(2,1)S(1)}, u32[]{:S(2)}, u32[]{:S(2)}) collective-permute-start(bf16[16,1,576]{2,1,0:T(2,128)(2,1)S(1)} %collective-permute-done.6), channel_id=1, source_target_pairs={{0,1},{1,2},{2,3},{3,4},{4,5},{5,6},{6,7},{7,8},{8,9},{9,10},{10,1... | collective-permute-start | bytes 55304 | tf_op jit(solution)/shard_map/ppermute | solution.py:20
  61.3 6.1 %collective-permute-start.8 = (bf16[16,1,576]{2,1,0:T(2,128)(2,1)S(1)}, bf16[16,1,576]{2,1,0:T(2,128)(2,1)S(1)}, u32[]{:S(2)}, u32[]{:S(2)}) collective-permute-start(bf16[16,1,576]{2,1,0:T(2,128)(2,1)S(1)} %collective-permute-done.7), channel_id=1, source_target_pairs={{0,1},{1,2},{2,3},{3,4},{4,5},{5,6},{6,7},{7,8},{8,9},{9,10},{10,1... | collective-permute-start | bytes 55304 | tf_op jit(solution)/shard_map/ppermute | solution.py:20
  67.4 6.1 %collective-permute-start.9 = (bf16[16,1,576]{2,1,0:T(2,128)(2,1)S(1)}, bf16[16,1,576]{2,1,0:T(2,128)(2,1)S(1)}, u32[]{:S(2)}, u32[]{:S(2)}) collective-permute-start(bf16[16,1,576]{2,1,0:T(2,128)(2,1)S(1)} %collective-permute-done.8), channel_id=1, source_target_pairs={{0,1},{1,2},{2,3},{3,4},{4,5},{5,6},{6,7},{7,8},{8,9},{9,10},{10,1... | collective-permute-start | bytes 55304 | tf_op jit(solution)/shard_map/ppermute | solution.py:20
  73.5 6.1 %collective-permute-start.10 = (bf16[16,1,576]{2,1,0:T(2,128)(2,1)S(1)}, bf16[16,1,576]{2,1,0:T(2,128)(2,1)S(1)}, u32[]{:S(2)}, u32[]{:S(2)}) collective-permute-start(bf16[16,1,576]{2,1,0:T(2,128)(2,1)S(1)} %collective-permute-done.9), channel_id=1, source_target_pairs={{0,1},{1,2},{2,3},{3,4},{4,5},{5,6},{6,7},{7,8},{8,9},{9,10},{10,1... | collective-permute-start | bytes 55304 | tf_op jit(solution)/shard_map/ppermute | solution.py:20
  79.7 6.1 %collective-permute-start.11 = (bf16[16,1,576]{2,1,0:T(2,128)(2,1)S(1)}, bf16[16,1,576]{2,1,0:T(2,128)(2,1)S(1)}, u32[]{:S(2)}, u32[]{:S(2)}) collective-permute-start(bf16[16,1,576]{2,1,0:T(2,128)(2,1)S(1)} %collective-permute-done.10), channel_id=1, source_target_pairs={{0,1},{1,2},{2,3},{3,4},{4,5},{5,6},{6,7},{7,8},{8,9},{9,10},{10,1... | collective-permute-start | bytes 55304 | tf_op jit(solution)/shard_map/ppermute | solution.py:20
  85.8 6.1 %collective-permute-start.12 = (bf16[16,1,576]{2,1,0:T(2,128)(2,1)S(1)}, bf16[16,1,576]{2,1,0:T(2,128)(2,1)S(1)}, u32[]{:S(2)}, u32[]{:S(2)}) collective-permute-start(bf16[16,1,576]{2,1,0:T(2,128)(2,1)S(1)} %collective-permute-done.11), channel_id=1, source_target_pairs={{0,1},{1,2},{2,3},{3,4},{4,5},{5,6},{6,7},{7,8},{8,9},{9,10},{10,1... | collective-permute-start | bytes 55304 | tf_op jit(solution)/shard_map/ppermute | solution.py:20
  91.9 6.1 %collective-permute-start.13 = (bf16[16,1,576]{2,1,0:T(2,128)(2,1)S(1)}, bf16[16,1,576]{2,1,0:T(2,128)(2,1)S(1)}, u32[]{:S(2)}, u32[]{:S(2)}) collective-permute-start(bf16[16,1,576]{2,1,0:T(2,128)(2,1)S(1)} %collective-permute-done.12), channel_id=1, source_target_pairs={{0,1},{1,2},{2,3},{3,4},{4,5},{5,6},{6,7},{7,8},{8,9},{9,10},{10,1... | collective-permute-start | bytes 55304 | tf_op jit(solution)/shard_map/ppermute | solution.py:20
  98.0 83.7 %collective-permute-start.14 = (bf16[16,1,576]{2,1,0:T(2,128)(2,1)S(1)}, bf16[16,1,576]{2,1,0:T(2,128)(2,1)S(1)}, u32[]{:S(2)}, u32[]{:S(2)}) collective-permute-start(bf16[16,1,576]{2,1,0:T(2,128)(2,1)S(1)} %collective-permute-done.13), channel_id=1, source_target_pairs={{0,1},{1,2},{2,3},{3,4},{4,5},{5,6},{6,7},{7,8},{8,9},{9,10},{10,1... | collective-permute-start | bytes 55304 | tf_op jit(solution)/shard_map/ppermute | solution.py:20
  224.0 61.5 %copy-start.1 = (s32[16,512]{1,0:T(8,128)S(1)}, s32[16,512]{1,0:T(8,128)}, u32[]{:S(2)}) copy-start(s32[16,512]{1,0:T(8,128)} %param.7) | copy-start | bytes 98308
  224.0 7.6 %copy-start.4 = (u32[32]{0:T(128)S(1)}, u32[32]{0:T(128)}, u32[]{:S(2)}) copy-start(u32[32]{0:T(128)} %constant.211) | copy-start | bytes 388
Sparse Core Ops, SparseCore 0:
  231.7 52.3 reduce-scatter.1
